TPU v7x, 32 devices: a whole 2x2x4 slice. The times are simulated.
32 devices in a mesh: dp: 8 (over y, x, core), mp: 4 (over z).
Axes of the slice: x: 2, y: 2, z: 4, core: 2. Of those that a mesh axis runs over, the one named last changes fastest.
Arguments:
- patches: bfloat16 [1024, 588], P('dp'), may hold values from -6 to 6
- embed_weight: bfloat16 [6144, 588], P(('mp', 'dp')), may hold values from -0.25 to 0.25
- project_weight: bfloat16 [6144, 3, 3072], P('dp', None, 'mp'), may hold values from -0.078125 to 0.078125
- patch_counts: int32 [64], P('dp'), may hold values from 0 to 64, as said below
- segment_ids: int32 [1024], P('dp'), may hold values from -1 to 63, as said below
- targets: bfloat16 [1024, 3072], P('dp', 'mp'), may hold values from -4 to 4
Outputs:
- project_grad: float32 [6144, 3, 3072], P('dp', None, 'mp')
- loss_value: float32 [], replicated
Inputs may be any that keep to these rules, and one draw needn't show every extreme that they name: `patch_counts`: entry 8 * i + j is the number of patches of image slot j of device i along dp, a multiple of 16, 0 for an empty slot; the counts of one device add up to at most 128, and some device reaches it. `segment_ids`: the rows of device i along dp hold its images whole, slot after slot, each row carrying the id 8 * i + slot of its image, then -1 on the rows left. A device in the upper half of dp holds more rows than the device half the axis away. On each device the images that end after its row 96 cover at most 64 rows. Those rows plus all the rows of the device half the axis away come to at most 96. Both bounds are reached.
All inputs are finite; a program needn't handle non-finite values.
Results may differ from a plain program's by a relative error of at most 0.012.
The roundings to bfloat16 on the way count: a program that leaves them out, or rounds other values in their place, can miss the bound.
Values may be sent and summed in bfloat16 or wider, within the bound.
A program may use at most 128 MiB of HBM per device.

v0:
```python
import math
import jax
import jax.numpy as jnp
from jax import lax
from jax.sharding import PartitionSpec as P

HD = 128


def layer_norm(values):
    center = values - jnp.mean(values, axis=-1, keepdims=True)
    spread = jnp.mean(center * center, axis=-1, keepdims=True)
    return center * lax.rsqrt(spread + 1e-06)


def norm_grad(values, cotangent):
    return jax.vjp(layer_norm, values)[1](cotangent)[0]


def attend_block(query_raw, key_raw, value_rows, segment, target):
    inverse_root = 1.0 / math.sqrt(HD)
    query_normed = layer_norm(query_raw).astype(jnp.bfloat16)
    key_normed = layer_norm(key_raw).astype(jnp.bfloat16)
    scores = (
        jnp.einsum("qhd,khd->hqk", query_normed, key_normed, preferred_element_type=jnp.float32)
        * inverse_root
    )
    valid = segment >= 0
    allowed = (segment[:, None] == segment[None, :]) & valid[:, None]
    exponent = jnp.where(allowed[None], jnp.exp(scores), 0.0)
    denominator = jnp.sum(exponent, axis=-1, keepdims=True)
    denominator = jnp.where(valid[None, :, None], denominator, 1.0)
    weights = (exponent / denominator).astype(jnp.bfloat16)
    attended = jnp.einsum("hqk,khd->qhd", weights, value_rows, preferred_element_type=jnp.float32)
    feature_count = attended.shape[1] * attended.shape[2]
    error_rows = jnp.where(
        valid[:, None], attended.reshape(-1, feature_count) - target.astype(jnp.float32), 0.0
    )
    squared_sum = jnp.sum(error_rows * error_rows)
    return (query_normed, key_normed, weights, error_rows, squared_sum)


def attend_back(
    query_raw, key_raw, query_normed, key_normed, value_rows, weights, error_rows, patch_total
):
    inverse_root = 1.0 / math.sqrt(HD)
    out_grad = (error_rows / patch_total).astype(jnp.bfloat16).reshape(query_normed.shape)
    prob_grad = jnp.einsum("qhd,khd->hqk", out_grad, value_rows, preferred_element_type=jnp.float32)
    value_grad = jnp.einsum(
        "hqk,qhd->khd", weights, out_grad, preferred_element_type=jnp.float32
    ).astype(jnp.bfloat16)
    weight_float = weights.astype(jnp.float32)
    score_grad = (
        weight_float
        * (prob_grad - jnp.sum(prob_grad * weight_float, axis=-1, keepdims=True))
        * inverse_root
    ).astype(jnp.bfloat16)
    normed_grad_q = jnp.einsum(
        "hqk,khd->qhd", score_grad, key_normed, preferred_element_type=jnp.float32
    )
    normed_grad_k = jnp.einsum(
        "hqk,qhd->khd", score_grad, query_normed, preferred_element_type=jnp.float32
    )
    query_grad = norm_grad(query_raw, normed_grad_q).astype(jnp.bfloat16)
    key_grad = norm_grad(key_raw, normed_grad_k).astype(jnp.bfloat16)
    return jnp.stack([query_grad, key_grad, value_grad], axis=1)


def local(patches, embed_weight, project_weight, patch_counts, segment_ids, targets):
    local_total = jnp.sum(patch_counts).astype(jnp.float32)
    patch_total = lax.psum(local_total, "dp")
    row_total = patches.shape[0]
    own_features = jnp.einsum(
        "rp,cp->rc",
        patches,
        lax.all_gather(embed_weight, "dp", axis=0, tiled=True),
        preferred_element_type=jnp.float32,
    ).astype(jnp.bfloat16)
    embedded = lax.all_gather(own_features, "mp", axis=1, tiled=True)
    normed = layer_norm(embedded.astype(jnp.float32)).astype(jnp.bfloat16)
    flat_weight = project_weight.reshape(project_weight.shape[0], -1)
    section = normed
    projected = jnp.dot(
        section,
        lax.all_gather(flat_weight, "dp", axis=0, tiled=True),
        preferred_element_type=jnp.float32,
    )
    head_dev = project_weight.shape[2] // HD
    projected = projected.reshape(row_total, 3, head_dev, HD)
    query_raw = projected[:, 0]
    key_raw = projected[:, 1]
    value_rows = projected[:, 2].astype(jnp.bfloat16)
    query_normed, key_normed, weights, error_rows, squared_sum = attend_block(
        query_raw, key_raw, value_rows, segment_ids, targets
    )
    loss_value = lax.psum(squared_sum, ("dp", "mp")) / (2.0 * patch_total)
    grad_rows = attend_back(
        query_raw, key_raw, query_normed, key_normed, value_rows, weights, error_rows, patch_total
    )
    grad_rows = grad_rows.reshape(row_total, -1)
    normed_blocks = lax.all_to_all(normed, "dp", split_axis=1, concat_axis=0, tiled=True)
    section = normed_blocks
    weight_grad = lax.dot_general(
        section,
        lax.all_gather(grad_rows, "dp", axis=0, tiled=True),
        (((0,), (0,)), ((), ())),
        preferred_element_type=jnp.float32,
    )
    return (weight_grad.reshape(weight_grad.shape[0], 3, -1), loss_value)


def solution(mesh):
    in_specs = (
        P("dp", None),
        P(("mp", "dp"), None),
        P("dp", None, "mp"),
        P("dp"),
        P("dp"),
        P("dp", "mp"),
    )
    out_specs = (P("dp", None, "mp"), P())
    return jax.shard_map(local, mesh=mesh, in_specs=in_specs, out_specs=out_specs, check_vma=False)
```

profile of v0, /device:TPU:0, one launch (start us, length us, event | category | flops | bytes accessed | tf_op | source)
XLA Modules:
  0.0 322.9 jit_solution(9939542595625254220)
XLA Ops:
  7.2 0.7 all-gather.5.cloned.1.call-update
  8.0 31.9 %all-gather.5.cloned.1.call-done = bf16[1536,588]{1,0:T(8,128)(2,1)} async-done(((bf16[192,588]{1,0:T(8,128)(2,1)}), bf16[1536,588]{1,0:T(8,128)(2,1)}) %all-gather.5.cloned.1.call-update) | async-done | bytes 1806352 | tf_op jit(solution)/shard_map/all_gather | solution.py:76
  39.9 3.1 convolution_convert_fusion
  43.0 6.0 %copy.36 = bf16[768,3,768]{0,2,1:T(8,128)(2,1)} copy(bf16[768,3,768]{2,0,1:T(8,128)(2,1)} %param.8) | data formatting | bytes 7077888 | tf_op args[2]
  49.1 0.6 copy-done.6
  49.7 0.6 reduce_sum.134
  51.0 14.4 %psum.14 = f32[]{:T(128)} all-reduce(f32[]{:T(128)S(6)} %convert_element_type.58), channel_id=1, replica_groups=mesh['dp'=8,'mp'=4] {'dp'}, use_global_device_ids=true, to_apply=%region_8.9 | all-reduce | flops 1 | bytes 8 | tf_op jit(solution)/shard_map/psum | solution.py:71
  65.4 0.2 copy.41
  65.6 0.1 compare_and_fusion
  65.7 14.5 %all-gather.7.cloned.1.call-done = bf16[128,6144]{1,0:T(8,128)(2,1)} async-done(((bf16[128,1536]{1,0:T(8,128)(2,1)}), bf16[128,6144]{1,0:T(8,128)(2,1)}) %all-gather.7.cloned.1.call-update) | async-done | bytes 1572880 | tf_op jit(solution)/shard_map/all_gather | solution.py:79
  80.2 1.8 convert_reduce_fusion
  82.0 0.1 copy-done.1
  82.0 0.6 fusion.3
  82.6 0.5 fusion.4
  83.1 136.3 %all-gather.9.cloned.1.call-done = bf16[6144,2304]{0,1:T(8,128)(2,1)} async-done(((bf16[768,2304]{0,1:T(8,128)(2,1)}), bf16[6144,2304]{0,1:T(8,128)(2,1)}) %all-gather.9.cloned.1.call-update) | async-done | bytes 28311568 | tf_op jit(solution)/shard_map/all_gather | solution.py:85
  219.4 12.7 %fusion.43 = f32[128,2304]{0,1:T(8,128)S(1)} fusion(bf16[128,6144]{1,0:T(8,128)(2,1)S(1)} %fusion.4, bf16[6144,2304]{0,1:T(8,128)(2,1)} %all-gather.9.cloned.1.call-done), kind=kOutput, calls=%fused_computation.75 | convolution fusion | flops 3623878656 | bytes 31064064 | tf_op jit(solution)/shard_map/dot_general | solution.py:83
  232.1 0.1 slice_reduce_fusion
  232.2 0.1 multiply_reduce_fusion.4
  232.3 0.3 fusion.38
  232.7 0.2 fusion.28
  232.9 1.4 multiply_reduce_fusion.1
  234.2 0.3 fusion.26
  234.5 0.9 fusion.11
  235.5 1.0 multiply_reduce_fusion.3
  236.5 1.6 fusion.30
  238.2 1.3 fusion.21
  239.5 0.1 fusion.22
  239.6 0.9 pad_maximum_fusion
  240.5 1.2 copy.59
  241.8 3.6 %all-to-all-start = ((bf16[128,8,768]{2,0,1:T(8,128)(2,1)}), bf16[128,8,768]{2,0,1:T(8,128)(2,1)S(1)}, u32[]{:S(2)}, u32[]{:S(2)}) async-start(bf16[128,8,768]{2,0,1:T(8,128)(2,1)} %bitcast.92), calls=%async_computation | async-start | bytes 3145728 | tf_op jit(solution)/shard_map/all_to_all | solution.py:101
  246.0 60.2 %psum.15 = f32[]{:T(128)} all-reduce(f32[]{:T(128)} %get-tuple-element.10), channel_id=1, replica_groups=mesh['dp'=8,'mp'=4] {'dp','mp'}, use_global_device_ids=true, to_apply=%region_15.16 | all-reduce | flops 1 | bytes 8 | tf_op jit(solution)/shard_map/psum | solution.py:96
  306.9 8.4 %fusion.44 = f32[768,3,768]{2,0,1:T(8,128)} fusion(bf16[1024,768,1]{1,0,2:T(8,128)(2,1)S(1)} %bitcast.107, bf16[3,768,1024]{2,1,0:T(8,128)(2,1)} %bitcast.108), kind=kOutput, calls=%fused_computation.76 | convolution fusion | flops 3623878656 | bytes 13369344 | tf_op jit(solution)/shard_map/dot_general | solution.py:103
  (33 shorter events, 0.4 us)
Async XLA Ops:
  7.2 32.7 %copy-start = (bf16[128,588]{0,1:T(8,128)(2,1)S(1)}, bf16[128,588]{0,1:T(8,128)(2,1)}, u32[]{:S(2)}) copy-start(bf16[128,588]{0,1:T(8,128)(2,1)} %param.6) | copy-start | bytes 451588
  7.2 32.7 %all-gather.5.cloned.1.call-start = ((), (), s32[]{:S(2)}) async-start(), calls=%async_computation.1 | async-start | bytes 2211840 | tf_op jit(solution)/shard_map/all_gather | solution.py:76
  7.9 72.3 %all-gather.7.cloned.1.call-start = ((), (), s32[]{:S(2)}) async-start(), calls=%async_computation.2 | async-start | bytes 1966080 | tf_op jit(solution)/shard_map/all_gather | solution.py:79
  43.0 176.4 %all-gather.9.cloned.1.call-start = ((), (), s32[]{:S(2)}) async-start(), calls=%async_computation.3 | async-start | bytes 31850496 | tf_op jit(solution)/shard_map/all_gather | solution.py:85
  49.1 0.7 copy-start.6
  49.1 16.3 %copy-start.4 = (bf16[128,768]{1,0:T(8,128)(2,1)S(1)}, bf16[128,768]{1,0:T(8,128)(2,1)}, u32[]{:S(2)}) copy-start(bf16[128,768]{1,0:T(8,128)(2,1)} %param.11) | copy-start | bytes 589828
  49.1 16.5 %copy-start.5 = (s32[128]{0:T(128)S(1)}, s32[128]{0:T(128)}, u32[]{:S(2)}) copy-start(s32[128]{0:T(128)} %param.10) | copy-start | bytes 1540
  49.1 257.8 %all-gather.11.cloned.1.call-start = ((), (), s32[]{:S(2)}) async-start(), calls=%async_computation.4 | async-start | bytes 5308416 | tf_op jit(solution)/shard_map/all_gather | solution.py:105
  80.2 1.9 copy-start.1
  234.5 2.0 copy-start.3
  238.1 1.4 copy-start.2
  241.8 65.1 %all-to-all-start = ((bf16[128,8,768]{2,0,1:T(8,128)(2,1)}), bf16[128,8,768]{2,0,1:T(8,128)(2,1)S(1)}, u32[]{:S(2)}, u32[]{:S(2)}) async-start(bf16[128,8,768]{2,0,1:T(8,128)(2,1)} %bitcast.92), calls=%async_computation | async-start | bytes 3145728 | tf_op jit(solution)/shard_map/all_to_all | solution.py:101
Sparse Core Ops, SparseCore 0:
  9.9 29.9 all-gather.4
  43.1 37.0 all-gather.6
  82.7 136.7 all-gather.8
  240.6 52.0 all-gather.10
where the time goes:
time: 324 us; the launch traced here: 323 us
  waiting for transfers between devices  183 us (56%)
  blocking collectives  74.6 us (23%)
  matrix products  28.5 us (9%)
  between operations  17.1 us (5%)
  local copies, waits for them, and re-layouts  8.09 us (2%)
  other arithmetic  7.53 us (2%)
  starting transfers between devices  3.74 us (1%)
    all_gather x1, waiting for transfers between devices, local(): lax.all_gather(flat_weight, 'dp', axis=0, tiled=True)  136 us
    psum x1, blocking collectives, local(): loss_value = lax.psum(squared_sum, ('dp', 'mp')) / (2.0 * patch_total)  60.2 us
    all_gather x1, waiting for transfers between devices, local(): lax.all_gather(embed_weight, 'dp', axis=0, tiled=True)  31.9 us
    all_gather x1, waiting for transfers between devices, local(): embedded = lax.all_gather(own_features, 'mp', axis=1, tiled=True)  14.5 us
    psum x1, blocking collectives, local(): patch_total = lax.psum(local_total, 'dp')  14.4 us
    dot_general x1, matrix products, local(): jnp.dot(section, lax.all_gather(flat_weight, 'dp', axis=0, tiled=True), p...  12.7 us
    dot_general x1, matrix products, local(): lax.dot_general(section, lax.all_gather(grad_rows, 'dp', axis=0, tiled=Tr...  8.4 us
    unnamed x16, local copies, waits for them, and re-layouts  6.84 us
  transfers between devices with their start and end apart: 5, of which 3 were waited for; matrix products, arithmetic and copies ran while one was open for 3% of the time, Pallas kernels for 0%

commit v1 on v0

--- a/solution.py
+++ b/solution.py
@@ -5,6 +5,17 @@
 from jax.sharding import PartitionSpec as P
 
 HD = 128
+
+
+def gather_around(array, axis, dim):
+    ways = lax.axis_size(axis)
+    pieces = [array]
+    for far in range(1, ways):
+        pieces.append(
+            lax.ppermute(pieces[far - 1], axis, [(d, (d - 1) % ways) for d in range(ways)])
+        )
+    line = jnp.concatenate(pieces, axis=dim)
+    return jnp.roll(line, lax.axis_index(axis) * array.shape[dim], axis=dim)
 
 
 def layer_norm(values):
@@ -81,9 +92,7 @@
     flat_weight = project_weight.reshape(project_weight.shape[0], -1)
     section = normed
     projected = jnp.dot(
-        section,
-        lax.all_gather(flat_weight, "dp", axis=0, tiled=True),
-        preferred_element_type=jnp.float32,
+        section, gather_around(flat_weight, "dp", 0), preferred_element_type=jnp.float32
     )
     head_dev = project_weight.shape[2] // HD
     projected = projected.reshape(row_total, 3, head_dev, HD)

time: 324 us -> 475 us (1.47)
  local copies, waits for them, and re-layouts: 8.09 us -> 63.4 us
  waiting for transfers between devices: 183 us -> 231 us
  blocking collectives: 74.6 us -> 97.8 us
  starting transfers between devices: 3.74 us -> 21.9 us
    ppermute x0 -> x7, waiting for transfers between devices: none -> 218 us  [gather_around(): lax.ppermute(pieces[far - 1], axis, [(d, (d - 1) % ways) for d in range(w...]
    all_gather x1 -> x0, waiting for transfers between devices: 136 us -> none  [local(): lax.all_gather(flat_weight, 'dp', axis=0, tiled=True)]
    unnamed x16 -> x45, local copies, waits for them, and re-layouts: 6.84 us -> 60 us
    psum x1, blocking collectives: 14.4 us -> 37.5 us  [local(): patch_total = lax.psum(local_total, 'dp')]
    all_gather x1, waiting for transfers between devices: 31.9 us -> 13.4 us  [local(): lax.all_gather(embed_weight, 'dp', axis=0, tiled=True)]
    ppermute x0 -> x7, starting transfers between devices: none -> 17.7 us  [gather_around(): lax.ppermute(pieces[far - 1], axis, [(d, (d - 1) % ways) for d in range(w...]
    all_gather x1, waiting for transfers between devices: 14.5 us -> 0.01 us  [local(): embedded = lax.all_gather(own_features, 'mp', axis=1, tiled=True)]
  transfers between devices with their start and end apart: 5 -> 11, of which waited for: 3 -> 7; matrix products, arithmetic and copies ran while one was open for 3% -> 7% of each run, Pallas kernels for 0% -> 0%
where the time goes in v1:
time: 475 us; the launch traced here: 474 us
  waiting for transfers between devices  231 us (49%)
  blocking collectives  97.8 us (21%)
  local copies, waits for them, and re-layouts  63.4 us (13%)
  matrix products  31.4 us (7%)
  starting transfers between devices  21.9 us (5%)
  between operations  17.1 us (4%)
  other arithmetic  11.2 us (2%)
    ppermute x7, waiting for transfers between devices, gather_around(): lax.ppermute(pieces[far - 1], axis, [(d, (d - 1) % ways) for d in range(w...  218 us
    psum x1, blocking collectives, local(): loss_value = lax.psum(squared_sum, ('dp', 'mp')) / (2.0 * patch_total)  60.3 us
    unnamed x45, local copies, waits for them, and re-layouts  60 us
    psum x1, blocking collectives, local(): patch_total = lax.psum(local_total, 'dp')  37.5 us
    ppermute x7, starting transfers between devices, gather_around(): lax.ppermute(pieces[far - 1], axis, [(d, (d - 1) % ways) for d in range(w...  17.7 us
    dot_general x1, matrix products, local(): jnp.dot(section, gather_around(flat_weight, 'dp', 0), preferred_element_t...  15.6 us
    all_gather x1, waiting for transfers between devices, local(): lax.all_gather(embed_weight, 'dp', axis=0, tiled=True)  13.4 us
  transfers between devices with their start and end apart: 11, of which 7 were waited for; matrix products, arithmetic and copies ran while one was open for 7% of the time, Pallas kernels for 0%

profile of v1, /device:TPU:0, one launch (start us, length us, event | category | flops | bytes accessed | tf_op | source)
XLA Modules:
  0.0 474.1 jit_solution(7020632375678065910)
XLA Ops:
  7.2 6.1 %copy.36 = bf16[768,3,768]{0,2,1:T(8,128)(2,1)} copy(bf16[768,3,768]{2,0,1:T(8,128)(2,1)} %param.8) | data formatting | bytes 7077888 | tf_op args[2]
  13.4 3.4 collective-permute-start
  16.7 39.3 %collective-permute-done = bf16[768,2304]{0,1:T(8,128)(2,1)S(1)} collective-permute-done((bf16[768,2304]{0,1:T(8,128)(2,1)}, bf16[768,2304]{0,1:T(8,128)(2,1)S(1)}, u32[]{:S(2)}, u32[]{:S(2)}) %collective-permute-start) | collective-permute-done | bytes 3538976 | tf_op jit(solution)/shard_map/ppermute | solution.py:15
  57.8 2.7 collective-permute-start.1
  60.5 39.0 %collective-permute-done.1 = bf16[768,2304]{0,1:T(8,128)(2,1)S(1)} collective-permute-done((bf16[768,2304]{0,1:T(8,128)(2,1)S(1)}, bf16[768,2304]{0,1:T(8,128)(2,1)S(1)}, u32[]{:S(2)}, u32[]{:S(2)}) %collective-permute-start.1) | collective-permute-done | bytes 3538976 | tf_op jit(solution)/shard_map/ppermute | solution.py:15
  101.3 2.8 collective-permute-start.2
  104.1 39.0 %collective-permute-done.2 = bf16[768,2304]{0,1:T(8,128)(2,1)S(1)} collective-permute-done((bf16[768,2304]{0,1:T(8,128)(2,1)S(1)}, bf16[768,2304]{0,1:T(8,128)(2,1)S(1)}, u32[]{:S(2)}, u32[]{:S(2)}) %collective-permute-start.2) | collective-permute-done | bytes 3538976 | tf_op jit(solution)/shard_map/ppermute | solution.py:15
  145.0 2.8 collective-permute-start.3
  147.8 39.0 %collective-permute-done.3 = bf16[768,2304]{0,1:T(8,128)(2,1)} collective-permute-done((bf16[768,2304]{0,1:T(8,128)(2,1)S(1)}, bf16[768,2304]{0,1:T(8,128)(2,1)}, u32[]{:S(2)}, u32[]{:S(2)}) %collective-permute-start.3) | collective-permute-done | bytes 3538976 | tf_op jit(solution)/shard_map/ppermute | solution.py:15
  186.8 2.9 collective-permute-start.4
  189.7 41.9 %collective-permute-done.4 = bf16[768,2304]{0,1:T(8,128)(2,1)} collective-permute-done((bf16[768,2304]{0,1:T(8,128)(2,1)}, bf16[768,2304]{0,1:T(8,128)(2,1)}, u32[]{:S(2)}, u32[]{:S(2)}) %collective-permute-start.4) | collective-permute-done | bytes 3538976 | tf_op jit(solution)/shard_map/ppermute | solution.py:15
  231.7 2.9 collective-permute-start.5
  234.5 13.4 %all-gather.4.cloned.1.call-done = bf16[1536,588]{1,0:T(8,128)(2,1)} async-done(((bf16[192,588]{1,0:T(8,128)(2,1)}), bf16[1536,588]{1,0:T(8,128)(2,1)}) %all-gather.4.cloned.1.call-update) | async-done | bytes 1806352 | tf_op jit(solution)/shard_map/all_gather | solution.py:87
  248.0 3.1 convolution_convert_fusion
  252.4 37.5 %psum.14 = f32[]{:T(128)} all-reduce(f32[]{:T(128)S(6)} %convert_element_type.58), channel_id=1, replica_groups=mesh['dp'=8,'mp'=4] {'dp'}, use_global_device_ids=true, to_apply=%region_8.9 | all-reduce | flops 1 | bytes 8 | tf_op jit(solution)/shard_map/psum | solution.py:82
  290.2 4.2 constant_dynamic-update-slice_fusion.15
  302.5 2.2 constant_dynamic-update-slice_fusion.13
  305.8 2.1 constant_dynamic-update-slice_fusion.12
  307.9 4.2 constant_dynamic-update-slice_fusion.11
  312.1 4.2 constant_dynamic-update-slice_fusion.10
  316.3 4.1 constant_dynamic-update-slice_fusion.9
  320.4 19.5 %collective-permute-done.6 = bf16[768,2304]{0,1:T(8,128)(2,1)S(1)} collective-permute-done((bf16[768,2304]{0,1:T(8,128)(2,1)}, bf16[768,2304]{0,1:T(8,128)(2,1)S(1)}, u32[]{:S(2)}, u32[]{:S(2)}) %collective-permute-start.6) | collective-permute-done | bytes 3538976 | tf_op jit(solution)/shard_map/ppermute | solution.py:15
  339.9 2.1 constant_dynamic-update-slice_fusion.8
  349.5 2.2 constant_dynamic-update-slice_fusion.4
  351.6 4.0 constant_dynamic-update-slice_fusion.3
  355.7 4.1 constant_dynamic-update-slice_fusion.2
  359.8 4.2 constant_dynamic-update-slice_fusion.1
  363.9 2.2 constant_dynamic-update-slice_fusion
  366.1 15.6 %fusion.1 = f32[128,2304]{0,1:T(8,128)S(1)} fusion(bf16[128,6144]{1,0:T(8,128)(2,1)S(1)} %fusion.6, bf16[12288,2304]{0,1:T(8,128)(2,1)} %constant_dynamic-update-slice_fusion, s32[]{:T(128)S(6)} %select_n.31), kind=kOutput, calls=%fused_computation.1 | convolution fusion | flops 3623878656 | bytes 31064068 | tf_op jit(solution)/shard_map/dot_general | solution.py:94
  392.2 4.1 all-to-all-start
  397.0 60.3 %psum.15 = f32[]{:T(128)} all-reduce(f32[]{:T(128)} %get-tuple-element.10), channel_id=1, replica_groups=mesh['dp'=8,'mp'=4] {'dp','mp'}, use_global_device_ids=true, to_apply=%region_15.16 | all-reduce | flops 1 | bytes 8 | tf_op jit(solution)/shard_map/psum | solution.py:105
  458.0 8.4 %fusion.46 = f32[768,3,768]{2,0,1:T(8,128)} fusion(bf16[1024,768,1]{1,0,2:T(8,128)(2,1)S(1)} %bitcast.108, bf16[3,768,1024]{2,1,0:T(8,128)(2,1)} %bitcast.109), kind=kOutput, calls=%fused_computation.94 | convolution fusion | flops 3623878656 | bytes 13369344 | tf_op jit(solution)/shard_map/dot_general | solution.py:112
  (74 shorter events, 33.5 us)
Async XLA Ops:
  7.2 240.8 %copy-start = (bf16[128,588]{0,1:T(8,128)(2,1)S(1)}, bf16[128,588]{0,1:T(8,128)(2,1)}, u32[]{:S(2)}) copy-start(bf16[128,588]{0,1:T(8,128)(2,1)} %param.6) | copy-start | bytes 451588
  7.2 243.9 %copy-start.13 = (s32[8]{0:T(128)S(1)}, s32[8]{0:T(128)}, u32[]{:S(2)}) copy-start(s32[8]{0:T(128)} %param.9) | copy-start | bytes 100
  7.2 282.7 %copy-start.11 = (bf16[128,768]{1,0:T(8,128)(2,1)S(1)}, bf16[128,768]{1,0:T(8,128)(2,1)}, u32[]{:S(2)}) copy-start(bf16[128,768]{1,0:T(8,128)(2,1)} %param.11) | copy-start | bytes 589828
  7.2 240.8 %all-gather.4.cloned.1.call-start = ((), (), s32[]{:S(2)}) async-start(), calls=%async_computation.1 | async-start | bytes 2211840 | tf_op jit(solution)/shard_map/all_gather | solution.py:87
  13.4 276.7 %copy-start.12 = (s32[128]{0:T(128)S(1)}, s32[128]{0:T(128)}, u32[]{:S(2)}) copy-start(s32[128]{0:T(128)} %param.10) | copy-start | bytes 1540
  13.4 42.7 %collective-permute-start = (bf16[768,2304]{0,1:T(8,128)(2,1)}, bf16[768,2304]{0,1:T(8,128)(2,1)S(1)}, u32[]{:S(2)}, u32[]{:S(2)}) collective-permute-start(bf16[768,2304]{0,1:T(8,128)(2,1)} %bitcast.92), channel_id=1, source_target_pairs={{0,28},{4,0},{8,4},{12,8},{16,12},{20,16},{24,20},{28,24},{1,29},{... | collective-permute-start | bytes 10616840 | tf_op jit(solution)/shard_map/ppermute | solution.py:15
  56.0 1.8 copy-start.3
  57.8 41.7 %collective-permute-start.1 = (bf16[768,2304]{0,1:T(8,128)(2,1)S(1)}, bf16[768,2304]{0,1:T(8,128)(2,1)S(1)}, u32[]{:S(2)}, u32[]{:S(2)}) collective-permute-start(bf16[768,2304]{0,1:T(8,128)(2,1)S(1)} %collective-permute-done), channel_id=1, source_target_pairs={{0,28},{4,0},{8,4},{12,8},{16,12},{20,16},{24,20},{28,24},{1,29},{... | collective-permute-start | bytes 10616840 | tf_op jit(solution)/shard_map/ppermute | solution.py:15
  99.5 1.8 copy-start.6
  101.3 41.8 %collective-permute-start.2 = (bf16[768,2304]{0,1:T(8,128)(2,1)S(1)}, bf16[768,2304]{0,1:T(8,128)(2,1)S(1)}, u32[]{:S(2)}, u32[]{:S(2)}) collective-permute-start(bf16[768,2304]{0,1:T(8,128)(2,1)S(1)} %collective-permute-done.1), channel_id=1, source_target_pairs={{0,28},{4,0},{8,4},{12,8},{16,12},{20,16},{24,20},{28,24},{1,29},{... | collective-permute-start | bytes 10616840 | tf_op jit(solution)/shard_map/ppermute | solution.py:15
  143.1 1.8 copy-start.8
  145.0 41.8 %collective-permute-start.3 = (bf16[768,2304]{0,1:T(8,128)(2,1)S(1)}, bf16[768,2304]{0,1:T(8,128)(2,1)}, u32[]{:S(2)}, u32[]{:S(2)}) collective-permute-start(bf16[768,2304]{0,1:T(8,128)(2,1)S(1)} %collective-permute-done.2), channel_id=1, source_target_pairs={{0,28},{4,0},{8,4},{12,8},{16,12},{20,16},{24,20},{28,24},{1,29},{... | collective-permute-start | bytes 10616840 | tf_op jit(solution)/shard_map/ppermute | solution.py:15
  186.8 44.9 %collective-permute-start.4 = (bf16[768,2304]{0,1:T(8,128)(2,1)}, bf16[768,2304]{0,1:T(8,128)(2,1)}, u32[]{:S(2)}, u32[]{:S(2)}) collective-permute-start(bf16[768,2304]{0,1:T(8,128)(2,1)} %collective-permute-done.3), channel_id=1, source_target_pairs={{0,28},{4,0},{8,4},{12,8},{16,12},{20,16},{24,20},{28,24},{1,29},{... | collective-permute-start | bytes 10616840 | tf_op jit(solution)/shard_map/ppermute | solution.py:15
  189.7 106.8 %all-gather.6.cloned.1.call-start = ((), (), s32[]{:S(2)}) async-start(), calls=%async_computation.2 | async-start | bytes 1966080 | tf_op jit(solution)/shard_map/all_gather | solution.py:90
  231.7 68.6 %collective-permute-start.5 = (bf16[768,2304]{0,1:T(8,128)(2,1)}, bf16[768,2304]{0,1:T(8,128)(2,1)}, u32[]{:S(2)}, u32[]{:S(2)}) collective-permute-start(bf16[768,2304]{0,1:T(8,128)(2,1)} %collective-permute-done.4), channel_id=1, source_target_pairs={{0,28},{4,0},{8,4},{12,8},{16,12},{20,16},{24,20},{28,24},{1,29},{... | collective-permute-start | bytes 10616840 | tf_op jit(solution)/shard_map/ppermute | solution.py:15
  251.1 206.9 %all-gather.8.cloned.1.call-start = ((), (), s32[]{:S(2)}) async-start(), calls=%async_computation.3 | async-start | bytes 5308416 | tf_op jit(solution)/shard_map/all_gather | solution.py:114
  290.2 4.2 copy-start.4
  296.5 6.0 %copy-start.7 = (bf16[768,2304]{0,1:T(8,128)(2,1)S(1)}, bf16[768,2304]{0,1:T(8,128)(2,1)}, u32[]{:S(2)}) copy-start(bf16[768,2304]{0,1:T(8,128)(2,1)} %copy-done.6) | copy-start | bytes 10616836
  300.3 39.6 %collective-permute-start.6 = (bf16[768,2304]{0,1:T(8,128)(2,1)}, bf16[768,2304]{0,1:T(8,128)(2,1)S(1)}, u32[]{:S(2)}, u32[]{:S(2)}) collective-permute-start(bf16[768,2304]{0,1:T(8,128)(2,1)} %collective-permute-done.5), channel_id=1, source_target_pairs={{0,28},{4,0},{8,4},{12,8},{16,12},{20,16},{24,20},{28,24},{1,29},{... | collective-permute-start | bytes 10616840 | tf_op jit(solution)/shard_map/ppermute | solution.py:15
  302.5 3.3 copy-start.9
  320.4 21.6 %copy-start.2 = (bf16[768,3,768]{0,2,1:T(8,128)(2,1)S(1)}, bf16[768,3,768]{0,2,1:T(8,128)(2,1)}, u32[]{:S(2)}) copy-start(bf16[768,3,768]{0,2,1:T(8,128)(2,1)} %copy.36) | copy-start | bytes 10616836
  342.0 3.3 copy-start.5
  384.1 2.0 copy-start.10
  392.2 65.7 %all-to-all-start = ((bf16[128,8,768]{2,0,1:T(8,128)(2,1)}), bf16[128,8,768]{2,0,1:T(8,128)(2,1)S(1)}, u32[]{:S(2)}, u32[]{:S(2)}) async-start(bf16[128,8,768]{2,0,1:T(8,128)(2,1)} %bitcast.91), calls=%async_computation | async-start | bytes 3145728 | tf_op jit(solution)/shard_map/all_to_all | solution.py:110
  458.0 8.4 %copy-start.1 = (bf16[128,588]{0,1:T(8,128)(2,1)S(1)}, bf16[128,588]{0,1:T(8,128)(2,1)}, u32[]{:S(2)}) copy-start(bf16[128,588]{0,1:T(8,128)(2,1)} %param.6) | copy-start | bytes 451588
Sparse Core Ops, SparseCore 0:
  189.8 58.1 all-gather.3
  251.2 37.0 all-gather.5
  391.1 52.7 all-gather.7
